TPU v7x, 256 devices: a whole 4x4x8 slice. The times are simulated.
256 devices in a mesh: freq: 4 (over z_lo), sub: 64 (over x, y, z_hi, core).
Axes of the slice: x: 4, y: 4, z: 8 (z_hi: 2, z_lo: 4; z = z_hi * 4 + z_lo), core: 2. Of those that a mesh axis runs over, the one named last changes fastest.
Arguments:
- sources: float32 [8, 4, 512, 64, 256], P('freq', None, 'sub'), may hold values from -5 to 5
- slowness: float32 [512, 64, 256], P('sub'), may hold values from 0.6 to 1.6
- freq_index: int32 [8], P('freq'), may hold values from 0 to 15
- coverage: int32 [4, 64, 64], P('freq'), may hold values from 0 to 511, as said below
Outputs:
- precond_gradient: float32 [512, 64, 256], P('sub', 'freq')
- delivered: float32 [4, 64, 64, 16, 256], P('freq', 'sub')
Inputs may be any that keep to these rules, and one draw needn't show every extreme that they name: `coverage`: each list names 64 distinct tiles of its depth band; a list names exactly 2 tiles of each owner it names and none of the others, so at most 2 of any one owner.
All inputs are finite; a program needn't handle non-finite values.
Results may differ from a plain program's by a relative error of at most 0.00002.
Values sent between devices are 32-bit elements; how exact they have to be, the bound alone decides.
A program may use at most 128 MiB of HBM per device.

v0:
```python
import jax
import jax.numpy as jnp
from jax import lax
from jax.sharding import PartitionSpec as P

PASSES = 4
TPD = 8
CAP = 2


def with_halo(array, sides, width):
    for axis, dim in sides:
        size, length = (lax.axis_size(axis), array.shape[dim])
        up = [(i, (i + 1) % size) for i in range(size - 1)]
        down = [(j, i) for i, j in up]
        last = lax.slice_in_dim(array, length - width, length, axis=dim)
        first = lax.slice_in_dim(array, 0, width, axis=dim)
        before = lax.ppermute(last, axis, up)
        after = lax.ppermute(first, axis, down)
        array = jnp.concatenate([before, array, after], axis=dim)
    return array


def smooth_axis(values, axis):
    widths = [(0, 0)] * values.ndim
    widths[axis] = (1, 1)
    padded = jnp.pad(values, widths)
    length = values.shape[axis]
    before = lax.slice_in_dim(padded, 0, length, axis=axis)
    middle = lax.slice_in_dim(padded, 1, length + 1, axis=axis)
    after = lax.slice_in_dim(padded, 2, length + 2, axis=axis)
    return 0.25 * before + 0.5 * middle + 0.25 * after


def across_smooth(extended):
    return 0.25 * extended[:, :, :-2] + 0.5 * extended[:, :, 1:-1] + 0.25 * extended[:, :, 2:]


def diagonal(sigma_cells):
    diag_real = 0.875 - sigma_cells
    return (diag_real, sigma_cells, diag_real * diag_real + sigma_cells * sigma_cells)


def combine(real_part, imag_part):
    joined = jnp.stack([real_part, imag_part], axis=2)
    return joined.reshape((joined.shape[0], 4) + joined.shape[3:])


def first_pass(forcing, diag_real, diag_imag, diag_norm):
    force_real = forcing[:, 0::2]
    force_imag = forcing[:, 1::2]
    real_coef = diag_real[:, None]
    imag_coef = diag_imag[:, None]
    norm_coef = diag_norm[:, None]
    real_part = (force_real * real_coef + force_imag * imag_coef) / norm_coef
    imag_part = (force_imag * real_coef - force_real * imag_coef) / norm_coef
    return combine(real_part, imag_part)


def relax(extended, forcing, sigma_cells, diag_real, diag_imag, diag_norm):
    smoothed = smooth_axis(smooth_axis(across_smooth(extended), 3), 4)
    inner = extended[:, :, 1:-1]
    real_part = inner[:, 0::2]
    imag_part = inner[:, 1::2]
    sigma_coef = sigma_cells[:, None]
    real_coef = diag_real[:, None]
    imag_coef = diag_imag[:, None]
    norm_coef = diag_norm[:, None]
    applied_real = real_part - sigma_coef * (real_part + imag_part) - smoothed[:, 0::2]
    applied_imag = imag_part - sigma_coef * (imag_part - real_part) - smoothed[:, 1::2]
    resid_real = forcing[:, 0::2] - applied_real
    resid_imag = forcing[:, 1::2] - applied_imag
    real_part = real_part + (resid_real * real_coef + resid_imag * imag_coef) / norm_coef
    imag_part = imag_part + (resid_imag * real_coef - resid_real * imag_coef) / norm_coef
    return combine(real_part, imag_part)


def body(sources, slowness, freq_index, coverage):
    groups = sources.shape[0]
    weights = 1.0 + freq_index.astype(jnp.float32) / 16.0
    scales = (0.12 * weights)[:, None, None, None]
    sigma_cells = scales * slowness[None]
    diag_real, diag_imag, diag_norm = diagonal(sigma_cells)
    fields = first_pass(sources, diag_real, diag_imag, diag_norm)
    for step in range(1, PASSES):
        padded = with_halo(fields.reshape((groups * 4,) + fields.shape[2:]), (("sub", 1),), 1)
        padded = padded.reshape((groups, 4) + padded.shape[1:])
        fields = relax(padded, sources, sigma_cells, diag_real, diag_imag, diag_norm)
    weight_coef = weights[:, None, None, None]
    grad_part = jnp.sum(
        weight_coef * (fields[:, 0] * fields[:, 2] - fields[:, 1] * fields[:, 3]), axis=0
    )
    illum_part = jnp.sum(
        weight_coef * (fields[:, 0] * fields[:, 0] + fields[:, 1] * fields[:, 1]), axis=0
    )
    grad_all, illum_all = lax.psum((grad_part, illum_part), "freq")
    depth = grad_all.shape[1] // lax.axis_size("freq")
    start = lax.axis_index("freq") * depth
    grad_share = lax.dynamic_slice_in_dim(grad_all, start, depth, 1)
    illum_share = lax.dynamic_slice_in_dim(illum_all, start, depth, 1)
    precond = grad_share / jnp.sqrt(illum_share + 1.0)
    tile_rows = precond.shape[1]
    members = lax.axis_size("sub")
    own_index = lax.axis_index("sub")
    lists = coverage[0]
    owner = lists // TPD
    local = lists % TPD
    position = jnp.arange(lists.shape[1], dtype=jnp.int32)
    same_owner = owner[:, :, None] == owner[:, None, :]
    earlier = position[None, :] < position[:, None]
    rank = jnp.sum((same_owner & earlier[None]).astype(jnp.int32), axis=2)
    mine = owner == own_index
    slots = jnp.arange(CAP, dtype=jnp.int32)
    hit = mine[:, :, None] & (rank[:, :, None] == slots[None, None, :])
    pick_tile = jnp.sum(jnp.where(hit, local[:, :, None], 0), axis=1)
    filled = jnp.any(hit, axis=1)
    outgoing = jnp.where(filled[:, :, None, None], precond[pick_tile], 0.0)
    incoming = lax.all_to_all(outgoing, "sub", split_axis=0, concat_axis=0, tiled=True)
    flat = incoming.reshape(members * CAP, tile_rows, precond.shape[2])
    own_owner = lax.dynamic_index_in_dim(owner, own_index, 0, keepdims=False)
    own_rank = lax.dynamic_index_in_dim(rank, own_index, 0, keepdims=False)
    delivered = flat[own_owner * CAP + own_rank]
    return (precond, delivered[None, None])


def solution(mesh):
    placed = (
        P("freq", None, "sub", None, None),
        P("sub", None, None),
        P("freq"),
        P("freq", None, None),
    )
    return jax.shard_map(
        body,
        mesh=mesh,
        in_specs=placed,
        out_specs=(P("sub", "freq", None), P("freq", "sub", None, None, None)),
        check_vma=False,
    )
```

profile of v0, /device:TPU:1, one launch (start us, length us, event | category | flops | bytes accessed | tf_op | source)
XLA Modules:
  0.0 313.5 jit_solution(3513300692828228335)
XLA Ops:
  7.9 1.5 multiply_subtract_fusion
  9.3 3.0 divide_bitcast_fusion.1
  12.9 10.2 %collective-permute-start = (f32[8,1,64,256]{3,2,1,0:T(8,128)S(1)}, f32[8,1,64,256]{3,2,1,0:T(8,128)S(1)}, u32[]{:S(2)}, u32[]{:S(2)}) collective-permute-start(f32[8,1,64,256]{3,2,1,0:T(8,128)S(1)} %get-tuple-element.23), channel_id=1, source_target_pairs={{0,1},{1,2},{2,3},{3,4},{4,5},{5,6},{6,7},{7,8},{8,9},{9,10},{10,1... | collective-permute-start | bytes 1572872 | tf_op jit(solution)/shard_map/ppermute | solution.py:18
  23.1 1.9 collective-permute-start.1
  25.0 7.0 %collective-permute-done = f32[8,1,64,256]{3,2,1,0:T(8,128)S(1)} collective-permute-done((f32[8,1,64,256]{3,2,1,0:T(8,128)S(1)}, f32[8,1,64,256]{3,2,1,0:T(8,128)S(1)}, u32[]{:S(2)}, u32[]{:S(2)}) %collective-permute-start) | collective-permute-done | bytes 524320 | tf_op jit(solution)/shard_map/ppermute | solution.py:18
  32.1 10.2 %collective-permute-done.1 = f32[8,1,64,256]{3,2,1,0:T(8,128)S(1)} collective-permute-done((f32[8,1,64,256]{3,2,1,0:T(8,128)S(1)}, f32[8,1,64,256]{3,2,1,0:T(8,128)S(1)}, u32[]{:S(2)}, u32[]{:S(2)}) %collective-permute-start.1) | collective-permute-done | bytes 524320 | tf_op jit(solution)/shard_map/ppermute | solution.py:19
  43.6 3.2 %fusion.2 = f32[2,4,8,64,256]{4,3,2,1,0:T(8,128)} fusion(f32[2,4,8,64,256]{4,3,2,1,0:T(8,128)S(1)} %fusion.33), kind=kLoop, calls=%fused_computation.16 | loop fusion | flops 5242880 | bytes 8388608 | tf_op jit(solution)/shard_map/add | solution.py:32
  46.8 9.0 %fusion.14 = f32[2,4,8,64,256]{4,3,2,1,0:T(8,128)} fusion(f32[2,4,8,64,256]{4,3,2,1,0:T(8,128)} %fusion.2), kind=kLoop, calls=%fused_computation.28 | loop fusion | flops 5242880 | bytes 8388608 | tf_op jit(solution)/shard_map/add | solution.py:32
  55.8 3.3 %add_bitcast_fusion.5 = (f32[2,2,1,8,64,256]{5,4,3,1,0,2:T(8,128)S(1)}, f32[2,2,8,64,256]{4,3,2,1,0:T(8,128)S(1)}, f32[2,2,8,64,256]{4,3,2,1,0:T(8,128)S(1)}) fusion(f32[2,4,8,64,256]{4,3,2,1,0:T(8,128)S(1)} %bitcast.125, f32[2,8,64,256]{3,2,1,0:T(8,128)S(1)} %get-tuple-element.26, f32[2,8,64,256]{3,2,1,0:T(8,128)S(1)} %get-tuple-element.27, ...), kind=kLoop, calls=%fused_computation.70 | loop fusion | flops 7864320 | bytes 22020096 | tf_op jit(solution)/shard_map/stack | solution.py:45
  61.0 1.9 collective-permute-start.2
  63.0 2.6 collective-permute-start.3
  65.6 3.5 %collective-permute-done.2 = f32[8,1,64,256]{3,2,1,0:T(8,128)S(1)} collective-permute-done((f32[8,1,64,256]{3,2,1,0:T(8,128)S(1)}, f32[8,1,64,256]{3,2,1,0:T(8,128)S(1)}, u32[]{:S(2)}, u32[]{:S(2)}) %collective-permute-start.2) | collective-permute-done | bytes 524320 | tf_op jit(solution)/shard_map/ppermute | solution.py:18
  69.1 22.4 %collective-permute-done.3 = f32[8,1,64,256]{3,2,1,0:T(8,128)S(1)} collective-permute-done((f32[8,1,64,256]{3,2,1,0:T(8,128)S(1)}, f32[8,1,64,256]{3,2,1,0:T(8,128)S(1)}, u32[]{:S(2)}, u32[]{:S(2)}) %collective-permute-start.3) | collective-permute-done | bytes 524320 | tf_op jit(solution)/shard_map/ppermute | solution.py:19
  92.8 3.2 %fusion.6 = f32[2,4,8,64,256]{4,3,2,1,0:T(8,128)} fusion(f32[2,4,8,64,256]{4,3,2,1,0:T(8,128)S(1)} %fusion.29), kind=kLoop, calls=%fused_computation.20 | loop fusion | flops 5242880 | bytes 8388608 | tf_op jit(solution)/shard_map/add | solution.py:32
  96.0 8.9 %fusion.18 = f32[2,4,8,64,256]{4,3,2,1,0:T(8,128)} fusion(f32[2,4,8,64,256]{4,3,2,1,0:T(8,128)} %fusion.6), kind=kLoop, calls=%fused_computation.32 | loop fusion | flops 5242880 | bytes 8388608 | tf_op jit(solution)/shard_map/add | solution.py:32
  104.9 3.3 %add_bitcast_fusion.3 = (f32[2,2,1,8,64,256]{5,4,3,1,0,2:T(8,128)S(1)}, f32[2,2,8,64,256]{4,3,2,1,0:T(8,128)S(1)}, f32[2,2,8,64,256]{4,3,2,1,0:T(8,128)S(1)}) fusion(f32[2,4,8,64,256]{4,3,2,1,0:T(8,128)S(1)} %bitcast.129, f32[2,8,64,256]{3,2,1,0:T(8,128)S(1)} %get-tuple-element.26, f32[2,8,64,256]{3,2,1,0:T(8,128)S(1)} %get-tuple-element.27, ...), kind=kLoop, calls=%fused_computation.66 | loop fusion | flops 7864320 | bytes 22020096 | tf_op jit(solution)/shard_map/stack | solution.py:45
  110.0 1.9 copy-done.2
  113.0 1.9 collective-permute-start.4
  115.0 3.5 %collective-permute-start.5 = (f32[8,1,64,256]{3,2,1,0:T(8,128)}, f32[8,1,64,256]{3,2,1,0:T(8,128)}, u32[]{:S(2)}, u32[]{:S(2)}) collective-permute-start(f32[8,1,64,256]{3,2,1,0:T(8,128)} %get-tuple-element.20), channel_id=1, source_target_pairs={{1,0},{2,1},{3,2},{4,3},{5,4},{6,5},{7,6},{8,7},{9,8},{10,9},{11,1... | collective-permute-start | bytes 1572872 | tf_op jit(solution)/shard_map/ppermute | solution.py:19
  118.4 3.0 collective-permute-done.4
  121.4 18.8 %collective-permute-done.5 = f32[8,1,64,256]{3,2,1,0:T(8,128)} collective-permute-done((f32[8,1,64,256]{3,2,1,0:T(8,128)}, f32[8,1,64,256]{3,2,1,0:T(8,128)}, u32[]{:S(2)}, u32[]{:S(2)}) %collective-permute-start.5) | collective-permute-done | bytes 524320 | tf_op jit(solution)/shard_map/ppermute | solution.py:19
  140.1 5.5 %fusion.25 = f32[2,4,8,64,256]{4,3,2,1,0:T(8,128)S(1)} fusion(f32[2,4,1,64,256]{4,3,2,1,0:T(8,128)} %bitcast.20, f32[2,4,8,64,256]{4,3,2,1,0:T(8,128)} %bitcast.120, f32[2,4,1,64,256]{4,3,2,1,0:T(8,128)} %bitcast.19), kind=kLoop, calls=%fused_computation.40 | loop fusion | flops 7340032 | bytes 9437184 | tf_op jit(solution)/shard_map/add | solution.py:36
  145.6 3.2 %fusion.10 = f32[2,4,8,64,256]{4,3,2,1,0:T(8,128)} fusion(f32[2,4,8,64,256]{4,3,2,1,0:T(8,128)S(1)} %fusion.25), kind=kLoop, calls=%fused_computation.24 | loop fusion | flops 5242880 | bytes 8388608 | tf_op jit(solution)/shard_map/add | solution.py:32
  148.8 9.0 %fusion.22 = f32[2,4,8,64,256]{4,3,2,1,0:T(8,128)} fusion(f32[2,4,8,64,256]{4,3,2,1,0:T(8,128)} %fusion.10), kind=kLoop, calls=%fused_computation.36 | loop fusion | flops 5242880 | bytes 8388608 | tf_op jit(solution)/shard_map/add | solution.py:32
  157.8 3.3 %add_bitcast_fusion.1 = (f32[2,2,1,8,64,256]{5,4,3,1,0,2:T(8,128)S(1)}, f32[2,2,8,64,256]{4,3,2,1,0:T(8,128)S(1)}, f32[2,2,8,64,256]{4,3,2,1,0:T(8,128)S(1)}) fusion(f32[2,4,8,64,256]{4,3,2,1,0:T(8,128)S(1)} %bitcast.121, f32[2,8,64,256]{3,2,1,0:T(8,128)S(1)} %get-tuple-element.26, f32[2,8,64,256]{3,2,1,0:T(8,128)S(1)} %get-tuple-element.27, ...), kind=kLoop, calls=%fused_computation.62 | loop fusion | flops 7864320 | bytes 22020096 | tf_op jit(solution)/shard_map/stack | solution.py:45
  163.1 1.6 fusion.39
  164.7 1.9 convert_reduce_fusion
  167.2 69.1 %all-reduce.9.cloned.1.call-done = (f32[8,64,256]{2,1,0:T(8,128)}, f32[8,64,256]{2,1,0:T(8,128)}) async-done(((f32[8,64,256]{2,1,0:T(8,128)}, f32[8,64,256]{2,1,0:T(8,128)}), (f32[8,64,256]{2,1,0:T(8,128)}, f32[8,64,256]{2,1,0:T(8,128)})) %all-reduce.9.cloned.1.call-update) | async-done | bytes 1048592 | tf_op jit(solution)/shard_map/psum | solution.py:96
  238.1 1.6 broadcast_select_fusion
  239.7 11.0 %all-to-all-start = ((f32[64,2,16,256]{3,2,1,0:T(8,128)}), f32[64,2,16,256]{3,2,1,0:T(8,128)S(1)}, u32[]{:S(2)}, u32[]{:S(2)}) async-start(f32[64,2,16,256]{3,2,1,0:T(8,128)} %broadcast_select_fusion), calls=%async_computation | async-start | bytes 4194304 | tf_op jit(solution)/shard_map/all_to_all | solution.py:118
  250.7 54.3 %all-to-all-done = f32[64,2,16,256]{3,2,1,0:T(8,128)S(1)} async-done(((f32[64,2,16,256]{3,2,1,0:T(8,128)}), f32[64,2,16,256]{3,2,1,0:T(8,128)S(1)}, u32[]{:S(2)}, u32[]{:S(2)}) %all-to-all-start) | async-done | bytes 2097184 | tf_op jit(solution)/shard_map/all_to_all | solution.py:118
  305.0 1.6 gather_fusion.1
  (42 shorter events, 13.2 us)
Async XLA Ops:
  7.2 229.2 %all-reduce.9.cloned.1.call-start = ((), (), s32[]{:S(2)}) async-start(), calls=%async_computation.1 | async-start | bytes 2097152 | tf_op jit(solution)/shard_map/psum | solution.py:96
  12.9 19.2 %collective-permute-start = (f32[8,1,64,256]{3,2,1,0:T(8,128)S(1)}, f32[8,1,64,256]{3,2,1,0:T(8,128)S(1)}, u32[]{:S(2)}, u32[]{:S(2)}) collective-permute-start(f32[8,1,64,256]{3,2,1,0:T(8,128)S(1)} %get-tuple-element.23), channel_id=1, source_target_pairs={{0,1},{1,2},{2,3},{3,4},{4,5},{5,6},{6,7},{7,8},{8,9},{9,10},{10,1... | collective-permute-start | bytes 1572872 | tf_op jit(solution)/shard_map/ppermute | solution.py:18
  23.1 19.2 %collective-permute-start.1 = (f32[8,1,64,256]{3,2,1,0:T(8,128)S(1)}, f32[8,1,64,256]{3,2,1,0:T(8,128)S(1)}, u32[]{:S(2)}, u32[]{:S(2)}) collective-permute-start(f32[8,1,64,256]{3,2,1,0:T(8,128)S(1)} %get-tuple-element.24), channel_id=1, source_target_pairs={{1,0},{2,1},{3,2},{4,3},{5,4},{6,5},{7,6},{8,7},{9,8},{10,9},{11,1... | collective-permute-start | bytes 1572872 | tf_op jit(solution)/shard_map/ppermute | solution.py:19
  46.8 9.0 %copy-start = (f32[2,4,8,64,256]{4,3,2,1,0:T(8,128)S(1)}, f32[2,4,8,64,256]{4,3,2,1,0:T(8,128)}, u32[]{:S(2)}) copy-start(f32[2,4,8,64,256]{4,3,2,1,0:T(8,128)} %param.4) | copy-start | bytes 12582916
  61.0 8.0 %collective-permute-start.2 = (f32[8,1,64,256]{3,2,1,0:T(8,128)S(1)}, f32[8,1,64,256]{3,2,1,0:T(8,128)S(1)}, u32[]{:S(2)}, u32[]{:S(2)}) collective-permute-start(f32[8,1,64,256]{3,2,1,0:T(8,128)S(1)} %get-tuple-element.21), channel_id=1, source_target_pairs={{0,1},{1,2},{2,3},{3,4},{4,5},{5,6},{6,7},{7,8},{8,9},{9,10},{10,1... | collective-permute-start | bytes 1572872 | tf_op jit(solution)/shard_map/ppermute | solution.py:18
  63.0 28.5 %collective-permute-start.3 = (f32[8,1,64,256]{3,2,1,0:T(8,128)S(1)}, f32[8,1,64,256]{3,2,1,0:T(8,128)S(1)}, u32[]{:S(2)}, u32[]{:S(2)}) collective-permute-start(f32[8,1,64,256]{3,2,1,0:T(8,128)S(1)} %get-tuple-element.22), channel_id=1, source_target_pairs={{1,0},{2,1},{3,2},{4,3},{5,4},{6,5},{7,6},{8,7},{9,8},{10,9},{11,1... | collective-permute-start | bytes 1572872 | tf_op jit(solution)/shard_map/ppermute | solution.py:19
  110.0 2.0 copy-start.2
  113.0 8.3 %collective-permute-start.4 = (f32[8,1,64,256]{3,2,1,0:T(8,128)}, f32[8,1,64,256]{3,2,1,0:T(8,128)}, u32[]{:S(2)}, u32[]{:S(2)}) collective-permute-start(f32[8,1,64,256]{3,2,1,0:T(8,128)} %get-tuple-element.19), channel_id=1, source_target_pairs={{0,1},{1,2},{2,3},{3,4},{4,5},{5,6},{6,7},{7,8},{8,9},{9,10},{10,1... | collective-permute-start | bytes 1572872 | tf_op jit(solution)/shard_map/ppermute | solution.py:18
  115.0 25.2 %collective-permute-start.5 = (f32[8,1,64,256]{3,2,1,0:T(8,128)}, f32[8,1,64,256]{3,2,1,0:T(8,128)}, u32[]{:S(2)}, u32[]{:S(2)}) collective-permute-start(f32[8,1,64,256]{3,2,1,0:T(8,128)} %get-tuple-element.20), channel_id=1, source_target_pairs={{1,0},{2,1},{3,2},{4,3},{5,4},{6,5},{7,6},{8,7},{9,8},{10,9},{11,1... | collective-permute-start | bytes 1572872 | tf_op jit(solution)/shard_map/ppermute | solution.py:19
  148.8 9.0 %copy-start.1 = (f32[2,4,8,64,256]{4,3,2,1,0:T(8,128)S(1)}, f32[2,4,8,64,256]{4,3,2,1,0:T(8,128)}, u32[]{:S(2)}) copy-start(f32[2,4,8,64,256]{4,3,2,1,0:T(8,128)} %param.4) | copy-start | bytes 12582916
  148.8 9.0 %copy-start.3 = (f32[2,2,2,8,64,256]{5,4,3,2,1,0:T(8,128)S(1)}, f32[2,2,2,8,64,256]{5,4,3,2,1,0:T(8,128)}, u32[]{:S(2)}) copy-start(f32[2,2,2,8,64,256]{5,4,3,2,1,0:T(8,128)} %copy-done.2) | copy-start | bytes 12582916
  163.1 1.6 copy-start.5
  237.3 2.4 copy-start.4
  239.7 65.3 %all-to-all-start = ((f32[64,2,16,256]{3,2,1,0:T(8,128)}), f32[64,2,16,256]{3,2,1,0:T(8,128)S(1)}, u32[]{:S(2)}, u32[]{:S(2)}) async-start(f32[64,2,16,256]{3,2,1,0:T(8,128)} %broadcast_select_fusion), calls=%async_computation | async-start | bytes 4194304 | tf_op jit(solution)/shard_map/all_to_all | solution.py:118
Sparse Core Ops, SparseCore 0:
  164.8 71.4 all-reduce.8
where the time goes:
time: 314 us; the launch traced here: 313 us
  waiting for transfers between devices  188 us (60%)
  other arithmetic  70.4 us (22%)
  starting transfers between devices  33 us (11%)
  between operations  14.3 us (5%)
  local copies, waits for them, and re-layouts  7.44 us (2%)
    psum x1, waiting for transfers between devices, body(): grad_all, illum_all = lax.psum((grad_part, illum_part), 'freq')  69.1 us
    all_to_all x1, waiting for transfers between devices, body(): lax.all_to_all(outgoing, 'sub', split_axis=0, concat_axis=0, tiled=True)  54.3 us
    ppermute x3, waiting for transfers between devices, with_halo(): after = lax.ppermute(first, axis, down)  51.3 us
    add x6, other arithmetic, smooth_axis(): return 0.25 * before + 0.5 * middle + 0.25 * after  36.3 us
    another operation x11, other arithmetic, combine(): joined = jnp.stack([real_part, imag_part], axis=2)  17.4 us
    ppermute x3, starting transfers between devices, with_halo(): before = lax.ppermute(last, axis, up)  14 us
    ppermute x3, waiting for transfers between devices, with_halo(): before = lax.ppermute(last, axis, up)  13.5 us
    all_to_all x1, starting transfers between devices, body(): lax.all_to_all(outgoing, 'sub', split_axis=0, concat_axis=0, tiled=True)  11 us
  transfers between devices with their start and end apart: 8, of which 8 were waited for; matrix products, arithmetic and copies ran while one was open for 1% of the time, Pallas kernels for 0%

commit v1 on v0

v1 whole, which is shorter than its diff:
```python
import jax
import jax.numpy as jnp
from jax import lax
from jax.experimental import pallas as pl
from jax.experimental.pallas import tpu as pltpu
from jax.sharding import PartitionSpec as P

MESH = pl.DeviceIdType.MESH
CX = 8
BAND = 16
ROUNDS = ((3, 8), (2, 3), (1, 2), (0, 1))


def smooth_plane(t):
    rows, cols = t.shape
    row = lax.broadcasted_iota(jnp.int32, t.shape, 0)
    col = lax.broadcasted_iota(jnp.int32, t.shape, 1)
    before = jnp.where(row == 0, 0.0, pltpu.roll(t, 1, 0))
    after = jnp.where(row == rows - 1, 0.0, pltpu.roll(t, rows - 1, 0))
    t = before + after + (t + t)
    before = jnp.where(col == 0, 0.0, pltpu.roll(t, 1, 1))
    after = jnp.where(col == cols - 1, 0.0, pltpu.roll(t, cols - 1, 1))
    return before + after + (t + t)


def kernel(
    src_hbm, slow_hbm, freq_ref, cover_ref, pre_ref, deliv_ref,
    src, slow, coef, v, halo, slow_x, coef_x, corr, gi, rsr, ag,
    load_sem, slow_sem, halo_ssem, halo_rsem, sx_ssem, sx_rsem, core_ssem, core_rsem,
    rs_ssem, rs_rsem, z_ssem, z_rsem, p1_ssem, p1_rsem, p2_ssem, p2_rsem, cc_ssem, cc_rsem,
):
    f = lax.axis_index("freq")
    s = lax.axis_index("sub")
    c = lax.rem(s, 2)
    zh = lax.rem(s // 2, 2)
    y = lax.rem(s // 4, 4)
    x = s // 16

    def dev(x_, y_, z_, c_):
        return {"freq": f, "sub": ((x_ * 4 + y_) * 2 + z_) * 2 + c_}

    def layer(m):
        return m + c * (CX - 1 - 2 * m)

    x_dev = {"freq": f, "sub": lax.rem(s + 2 * c + 63, 64)}
    c_dev = dev(x, y, zh, 1 - c)
    z_dev = dev(x, y, 1 - zh, c)
    xs = [dev(lax.rem(x + k, 4), y, zh, c) for k in (1, 2, 3)]
    ys = [dev(x, lax.rem(y + k, 4), zh, c) for k in (1, 2, 3)]
    fs = [{"freq": lax.rem(f + k, 4), "sub": s} for k in (1, 2, 3)]
    has_x = jnp.where((s == 0) | (s == 63), 0.0, 1.0).astype(jnp.float32)
    quarter_x = has_x * (0.25 / 16.0)

    slow_loads = [
        pltpu.make_async_copy(slow_hbm.at[layer(m)], slow.at[m], slow_sem.at[m]) for m in range(CX)
    ]
    loads = [
        pltpu.make_async_copy(src_hbm.at[:, :, layer(m)], src.at[m], load_sem.at[m]) for m in range(CX)
    ]
    for m in (0, 1, 2, 7, 3, 4, 5, 6):
        slow_loads[m].start()
        loads[m].start()

    barrier = pltpu.get_barrier_semaphore()
    partners = [x_dev, c_dev, z_dev] + xs + ys + fs
    for who in partners:
        pl.semaphore_signal(barrier, inc=1, device_id=who, device_id_type=MESH)

    weights = [1.0 + freq_ref[g].astype(jnp.float32) / 16.0 for g in range(2)]

    def remote(src_ref, dst_ref, ssem, rsem, who):
        return pltpu.make_async_remote_copy(
            src_ref=src_ref, dst_ref=dst_ref, send_sem=ssem, recv_sem=rsem,
            device_id=who, device_id_type=MESH,
        )

    def coefs(sigma):
        real = 0.875 - sigma
        inv = 1.0 / (real * real + sigma * sigma)
        return real * inv, sigma * inv

    def over_fields(step):
        def one(i, carry):
            step(i // 2, lax.rem(i, 2) * 2)
            return carry
        lax.fori_loop(0, 4, one, 0)

    def put(ref, where, g, q, h, cr, ci, add=False):
        real = h[0] * cr + h[1] * ci
        imag = h[1] * cr - h[0] * ci
        if add:
            real = real + ref[where + (g, q)]
            imag = imag + ref[where + (g, q + 1)]
        ref[where + (g, q)] = real
        ref[where + (g, q + 1)] = imag

    def first(m):
        for g in range(2):
            cr, ci = coefs((0.12 * weights[g]) * slow[m])
            coef[m, g, 0] = cr
            coef[m, g, 1] = ci
            for q in (0, 2):
                put(v, (0, m + 1), g, q, (src[m, g, q], src[m, g, q + 1]), cr, ci)

    def relax(level, m):
        def step(g, q):
            h = []
            for part in (0, 1):
                mid = v[level, m + 1, g, q + part]
                t = v[level, m, g, q + part] + v[level, m + 2, g, q + part] + (mid + mid)
                h.append(src[m, g, q + part] + (smooth_plane(t) * (1.0 / 64.0) - 0.125 * mid))
            put(v, (level + 1, m + 1), g, q, h, coef[m, g, 0], coef[m, g, 1])
        over_fields(step)

    def relax_range(level, lo, hi):
        def one(m, carry):
            relax(level, m)
            return carry
        lax.fori_loop(lo, hi, one, 0)

    def first_range(lo, hi):
        def one(m, carry):
            first(m)
            return carry
        lax.fori_loop(lo, hi, one, 0)

    for level in range(3):
        def clear(i, carry):
            v[level, 0, i // 4, lax.rem(i, 4)] = jnp.zeros((64, 256), jnp.float32)
            return carry
        lax.fori_loop(0, 8, clear, 0)

    x_sends = [
        remote(v.at[n, 1], halo.at[n], halo_ssem.at[n], halo_rsem.at[n], x_dev) for n in range(3)
    ]
    slow_send = remote(slow.at[0], slow_x, sx_ssem, sx_rsem, x_dev)
    c_sends = [
        remote(v.at[n, 8], v.at[n, 9], core_ssem.at[n], core_rsem.at[n], c_dev) for n in range(3)
    ]

    for m in (0, 1, 2):
        slow_loads[m].wait()
        loads[m].wait()
        if m == 0:
            first(0)
            pl.semaphore_wait(barrier, len(partners))
            x_sends[0].start()
            slow_send.start()
        elif m == 1:
            first(1)
            relax(0, 0)
            x_sends[1].start()
        else:
            first(2)
            relax(0, 1)
            relax(1, 0)
            x_sends[2].start()

    for m in (7, 3, 4, 5, 6):
        slow_loads[m].wait()
        loads[m].wait()
        if m == 7:
            first_range(7, 8)
            c_sends[0].start()
    first_range(3, 7)
    for level in range(3):
        c_sends[level].wait_recv()
        relax_range(level, 7, 8)
        if level < 2:
            c_sends[level + 1].start()
        relax_range(level, 2 - level, 7)

    def finish(lo, hi):
        def one(m, carry):
            for b in range(4):
                rows = pl.ds(b * BAND, BAND)
                grad = None
                for g in range(2):
                    ur, ui, ar, ai = [v[3, m + 1, g, q, rows, :] for q in range(4)]
                    gg = weights[g] * (ur * ar - ui * ai)
                    ii = weights[g] * (ur * ur + ui * ui)
                    grad, illum = (gg, ii) if grad is None else (grad + gg, illum + ii)
                gi[b, m, 0] = grad
                gi[b, m, 1] = illum
            return carry
        lax.fori_loop(lo, hi, one, 0)

    sent = []

    def rs_copies(r):
        lo, hi = ROUNDS[r]
        n = pl.ds(lo, hi - lo)
        return [
            remote(gi.at[lax.rem(f + k + 1, 4), n], rsr.at[k, n],
                   rs_ssem.at[r, k], rs_rsem.at[r, k], fs[k])
            for k in range(3)
        ]

    def block(r, *where):
        lo, hi = ROUNDS[r]
        return ag.at[where + (pl.ds(lo, hi - lo),)]

    def z_copy(r):
        b = block(r, x, y, zh, c)
        return remote(b, b, z_ssem.at[r], z_rsem.at[r], z_dev)

    def p1_copies(r, flow):
        b = block(r, x, y, zh, c) if flow == 0 else block(r, x, y, 1 - zh, c)
        to = xs if flow == 0 else ys
        return [remote(b, b, p1_ssem.at[flow, r, k], p1_rsem.at[flow, r, k], to[k]) for k in range(3)]

    every = slice(None)

    def p2_copies(r, flow):
        b = block(r, every, y, zh, c) if flow == 0 else block(r, x, every, 1 - zh, c)
        to = ys if flow == 0 else xs
        return [remote(b, b, p2_ssem.at[flow, r, k], p2_rsem.at[flow, r, k], to[k]) for k in range(3)]

    def cc_copy(r):
        b = block(r, every, every, every, c)
        return remote(b, b, cc_ssem.at[r], cc_rsem.at[r], c_dev)

    def start(copies):
        for copy in copies:
            copy.start()
            sent.append(copy)

    def arrived(copies):
        for copy in copies:
            copy.wait_recv()

    def reduce_start(r):
        finish(*ROUNDS[r])
        start(rs_copies(r))

    def gather_start(r):
        arrived(rs_copies(r))
        lo, hi = ROUNDS[r]

        def one(m, carry):
            grad = gi[f, m, 0] + rsr[0, m, 0] + rsr[1, m, 0] + rsr[2, m, 0]
            illum = gi[f, m, 1] + rsr[0, m, 1] + rsr[1, m, 1] + rsr[2, m, 1]
            pre = grad / jnp.sqrt(illum + 1.0)
            ag[x, y, zh, c, m] = pre
            pre_ref[layer(m)] = pre
            return carry
        lax.fori_loop(lo, hi, one, 0)
        start([z_copy(r)])
        start(p1_copies(r, 0))

    def gather_middle(r):
        arrived([z_copy(r)])
        start(p1_copies(r, 1))
        arrived(p1_copies(r, 0))
        start(p2_copies(r, 0))
        arrived(p1_copies(r, 1))
        start(p2_copies(r, 1))

    def gather_end(r):
        arrived(p2_copies(r, 0))
        arrived(p2_copies(r, 1))
        start([cc_copy(r)])

    C2, C3A, C3B, D2, D3 = range(5)

    def correct(ref, where, cf, terms, minus=None, add=False):
        def step(g, q):
            h = []
            for part in (0, 1):
                t = None
                for scale, tref, twhere in terms:
                    one = scale * tref[twhere + (g, q + part)]
                    t = one if t is None else t + one
                k = smooth_plane(t)
                if minus is not None:
                    k = k - 0.125 * minus[0][minus[1] + (g, q + part)]
                h.append(k)
            put(ref, where, g, q, h, cf[g, 0], cf[g, 1], add)
        over_fields(step)

    half = 0.5 / 16.0
    quarter = 0.25 / 16.0

    reduce_start(0)
    slow_send.wait_recv()
    for g in range(2):
        cr, ci = coefs((0.12 * weights[g]) * slow_x[...])
        coef_x[g, 0] = cr
        coef_x[g, 1] = ci
    correct(corr, (D2,), coef_x, [(quarter, v, (0, 1))])
    gather_start(0)

    x_sends[0].wait_recv()
    correct(corr, (C2,), coef.at[0], [(quarter_x, halo, (0,))])
    correct(corr, (C3B,), coef.at[1], [(quarter, corr, (C2,))])
    correct(v, (3, 3), coef.at[2], [(quarter, corr, (C3B,))], add=True)
    reduce_start(1)
    gather_middle(0)
    correct(corr, (D3,), coef_x, [(half, corr, (D2,)), (quarter, v, (1, 1)), (quarter, corr, (C2,))],
            minus=(corr, (D2,)))
    gather_start(1)
    gather_end(0)
    gather_middle(1)

    x_sends[1].wait_recv()
    correct(corr, (C3A,), coef.at[0],
            [(half, corr, (C2,)), (quarter_x, halo, (1,)), (quarter_x, corr, (D2,))],
            minus=(corr, (C2,)))
    correct(v, (3, 2), coef.at[1], [(half, corr, (C3B,)), (quarter, corr, (C3A,))],
            minus=(corr, (C3B,)), add=True)
    reduce_start(2)
    correct(v, (3, 1), coef.at[0],
            [(half, corr, (C3A,)), (quarter, corr, (C3B,)), (quarter_x, corr, (D3,))],
            minus=(corr, (C3A,)), add=True)
    gather_end(1)
    gather_start(2)
    gather_middle(2)
    gather_end(2)

    x_sends[2].wait_recv()
    correct(v, (3, 1), coef.at[0], [(quarter_x, halo, (2,))], add=True)
    reduce_start(3)
    gather_start(3)
    gather_middle(3)
    gather_end(3)
    for r in range(4):
        arrived([cc_copy(r)])

    def pick(k, carry):
        tile = cover_ref[0, s, k]
        o = tile // CX
        j = lax.rem(tile, CX)
        oc = lax.rem(o, 2)
        m = j + oc * (CX - 1 - 2 * j)
        deliv_ref[0, 0, k] = ag[o // 16, lax.rem(o // 4, 4), lax.rem(o // 2, 2), oc, m]
        return carry
    lax.fori_loop(0, deliv_ref.shape[2], pick, 0)

    for copy in x_sends + [slow_send] + c_sends + sent:
        copy.wait_send()


def body(sources, slowness, freq_index, coverage):
    groups, parts, cx, nz, ny = sources.shape
    f32 = jnp.float32
    tiles = coverage.shape[2]
    vm = pltpu.VMEM
    dma = pltpu.SemaphoreType.DMA
    field = (groups, parts, nz, ny)
    return pl.pallas_call(
        kernel,
        name="inversion_step",
        out_shape=(
            jax.ShapeDtypeStruct((cx, BAND, ny), f32),
            jax.ShapeDtypeStruct((1, 1, tiles, BAND, ny), f32),
        ),
        in_specs=[
            pl.BlockSpec(memory_space=pl.ANY),
            pl.BlockSpec(memory_space=pl.ANY),
            pl.BlockSpec(memory_space=pltpu.SMEM),
            pl.BlockSpec(memory_space=pltpu.SMEM),
        ],
        out_specs=(pl.BlockSpec(memory_space=pltpu.VMEM), pl.BlockSpec(memory_space=pltpu.VMEM)),
        scratch_shapes=[
            vm((cx,) + field, f32),
            vm((cx, nz, ny), f32),
            vm((cx, groups, 2, nz, ny), f32),
            vm((4, cx + 2) + field, f32),
            vm((3,) + field, f32),
            vm((nz, ny), f32),
            vm((groups, 2, nz, ny), f32),
            vm((5,) + field, f32),
            vm((4, cx, 2, BAND, ny), f32),
            vm((3, cx, 2, BAND, ny), f32),
            vm((4, 4, 2, 2, cx, BAND, ny), f32),
            dma((cx,)), dma((cx,)),
            dma((3,)), dma((3,)), dma, dma, dma((3,)), dma((3,)),
            dma((4, 3)), dma((4, 3)), dma((4,)), dma((4,)),
            dma((2, 4, 3)), dma((2, 4, 3)), dma((2, 4, 3)), dma((2, 4, 3)),
            dma((4,)), dma((4,)),
        ],
        compiler_params=pltpu.CompilerParams(
            collective_id=0, has_side_effects=True, vmem_limit_bytes=60 << 20
        ),
    )(sources, slowness, freq_index, coverage)


def solution(mesh):
    placed = (
        P("freq", None, "sub", None, None),
        P("sub", None, None),
        P("freq"),
        P("freq", None, None),
    )
    return jax.shard_map(
        body,
        mesh=mesh,
        in_specs=placed,
        out_specs=(P("sub", "freq", None), P("freq", "sub", None, None, None)),
        check_vma=False,
    )
```

time: 314 us -> 185 us (0.59)
  waiting for transfers between devices: 188 us -> 0 us
  Pallas kernels: 0 us -> 181 us
  other arithmetic: 70.4 us -> 0 us
  starting transfers between devices: 33 us -> 0 us
  between operations: 14.3 us -> 0.64 us
  local copies, waits for them, and re-layouts: 7.44 us -> 3.83 us
    pallas_call x0 -> x1, Pallas kernels: none -> 181 us  [body(): pl.pallas_call(kernel, name='inversion_step', out_shape=(jax.ShapeDtypeSt...]
    psum x1 -> x0, waiting for transfers between devices: 69.1 us -> none  [body(): grad_all, illum_all = lax.psum((grad_part, illum_part), 'freq')]
    ppermute x6 -> x0, waiting for transfers between devices: 64.8 us -> none  [the longest x3 51.3 us: with_halo(): after = lax.ppermute(first, axis, down)]
    all_to_all x1 -> x0, waiting for transfers between devices: 54.3 us -> none  [body(): lax.all_to_all(outgoing, 'sub', split_axis=0, concat_axis=0, tiled=True)]
    add x10 -> x0, other arithmetic: 45.2 us -> none  [the longest x6 36.3 us: smooth_axis(): return 0.25 * before + 0.5 * middle + 0.25 * after]
    ppermute x6 -> x0, starting transfers between devices: 22 us -> none  [the longest x3 14 us: with_halo(): before = lax.ppermute(last, axis, up)]
    another operation x11 -> x0, other arithmetic: 17.4 us -> none  [combine(): joined = jnp.stack([real_part, imag_part], axis=2)]
    all_to_all x1 -> x0, starting transfers between devices: 11 us -> none  [body(): lax.all_to_all(outgoing, 'sub', split_axis=0, concat_axis=0, tiled=True)]
  transfers between devices with their start and end apart: 8 -> 0, of which waited for: 8 -> 0; matrix products, arithmetic and copies ran while one was open for 1% -> 0% of each run, Pallas kernels for 0% -> 0%
where the time goes in v1:
time: 185 us
  Pallas kernels  181 us (98%)
  local copies, waits for them, and re-layouts  3.83 us (2%)
    pallas_call x1, Pallas kernels, body(): pl.pallas_call(kernel, name='inversion_step', out_shape=(jax.ShapeDtypeSt...  181 us
    unnamed x2, local copies, waits for them, and re-layouts  3.83 us

profile of v1, /device:TPU:1, one launch (start us, length us, event | category | flops | bytes accessed | tf_op | source)
XLA Modules:
  0.0 185.1 jit_solution(2981924495787461997)
XLA Ops:
  0.6 180.6 %inversion_step.1 = (f32[8,16,256]{2,1,0:T(8,128)}, f32[1,1,64,16,256]{4,3,2,1,0:T(8,128)}) custom-call(f32[2,4,8,64,256]{4,3,2,1,0:T(8,128)} %src_hbm.1, f32[8,64,256]{2,1,0:T(8,128)} %slow_hbm.1, s32[2]{0:T(128)} %freq_ref.1, s32[1,64,64]{2,1,0:T(8,128)} %cover_ref.1), custom_call_target="tpu_custom_call" | custom-call | tf_op jit(solution)/shard_map/inversion_step/pallas_call | solution.py:350
  181.3 1.6 copy.8
  182.9 2.3 %copy.9 = f32[1,1,64,16,256]{4,3,2,1,0:T(8,128)} copy(f32[1,1,64,16,256]{4,3,2,1,0:T(8,128)} %get-tuple-element.5) | data formatting | bytes 2097152

commit v2 on v1

--- a/solution.py
+++ b/solution.py
@@ -8,7 +8,8 @@
 MESH = pl.DeviceIdType.MESH
 CX = 8
 BAND = 16
-ROUNDS = ((3, 8), (2, 3), (1, 2), (0, 1))
+REDUCE = ((3, 8), (2, 3), (1, 2), (0, 1))
+GATHER = ((2, 8), (1, 2), (0, 1))
 
 
 def smooth_plane(t):
@@ -131,9 +132,15 @@
         lax.fori_loop(0, 8, clear, 0)
 
     x_sends = [
-        remote(v.at[n, 1], halo.at[n], halo_ssem.at[n], halo_rsem.at[n], x_dev) for n in range(3)
+        [remote(v.at[n, 1, g], halo.at[n, g], halo_ssem.at[n, g], halo_rsem.at[n, g], x_dev) for g in range(2)]
+        for n in range(3)
     ]
-    slow_send = remote(slow.at[0], slow_x, sx_ssem, sx_rsem, x_dev)
+    quarter_rows = pl.ds(pl.multiple_of(f * BAND, BAND), BAND)
+    slow_send = remote(slow.at[0, quarter_rows], slow_x.at[quarter_rows], sx_ssem.at[0], sx_rsem.at[0], x_dev)
+    slow_shares = [
+        remote(slow_x.at[quarter_rows], slow_x.at[quarter_rows], sx_ssem.at[1 + k], sx_rsem.at[1 + k], fs[k])
+        for k in range(3)
+    ]
     c_sends = [
         remote(v.at[n, 8], v.at[n, 9], core_ssem.at[n], core_rsem.at[n], c_dev) for n in range(3)
     ]
@@ -144,17 +151,16 @@
         if m == 0:
             first(0)
             pl.semaphore_wait(barrier, len(partners))
-            x_sends[0].start()
             slow_send.start()
+            x_sends[0][0].start()
+            x_sends[0][1].start()
         elif m == 1:
             first(1)
             relax(0, 0)
-            x_sends[1].start()
         else:
             first(2)
             relax(0, 1)
             relax(1, 0)
-            x_sends[2].start()
 
     for m in (7, 3, 4, 5, 6):
         slow_loads[m].wait()
@@ -168,7 +174,7 @@
         relax_range(level, 7, 8)
         if level < 2:
             c_sends[level + 1].start()
-        relax_range(level, 2 - level, 7)
+        relax_range(level, 3 if level == 2 else 2 - level, 7)
 
     def finish(lo, hi):
         def one(m, carry):
@@ -188,7 +194,7 @@
     sent = []
 
     def rs_copies(r):
-        lo, hi = ROUNDS[r]
+        lo, hi = REDUCE[r]
         n = pl.ds(lo, hi - lo)
         return [
             remote(gi.at[lax.rem(f + k + 1, 4), n], rsr.at[k, n],
@@ -197,7 +203,7 @@
         ]
 
     def block(r, *where):
-        lo, hi = ROUNDS[r]
+        lo, hi = GATHER[r]
         return ag.at[where + (pl.ds(lo, hi - lo),)]
 
     def z_copy(r):
@@ -216,9 +222,15 @@
         to = ys if flow == 0 else xs
         return [remote(b, b, p2_ssem.at[flow, r, k], p2_rsem.at[flow, r, k], to[k]) for k in range(3)]
 
-    def cc_copy(r):
-        b = block(r, every, every, every, c)
-        return remote(b, b, cc_ssem.at[r], cc_rsem.at[r], c_dev)
+    def cc_copies(r, flow):
+        out = []
+        for k in range(4):
+            if flow == 0:
+                b = block(r, every, lax.rem(y + 4 - k, 4), zh, c)
+            else:
+                b = block(r, lax.rem(x + 4 - k, 4), every, 1 - zh, c)
+            out.append(remote(b, b, cc_ssem.at[flow, r, k], cc_rsem.at[flow, r, k], c_dev))
+        return out
 
     def start(copies):
         for copy in copies:
@@ -230,12 +242,13 @@
             copy.wait_recv()
 
     def reduce_start(r):
-        finish(*ROUNDS[r])
+        finish(*REDUCE[r])
         start(rs_copies(r))
 
     def gather_start(r):
-        arrived(rs_copies(r))
-        lo, hi = ROUNDS[r]
+        for i in (0, 1) if r == 0 else (r + 1,):
+            arrived(rs_copies(i))
+        lo, hi = GATHER[r]
 
         def one(m, carry):
             grad = gi[f, m, 0] + rsr[0, m, 0] + rsr[1, m, 0] + rsr[2, m, 0]
@@ -253,13 +266,18 @@
         start(p1_copies(r, 1))
         arrived(p1_copies(r, 0))
         start(p2_copies(r, 0))
+        start(cc_copies(r, 0)[:1])
         arrived(p1_copies(r, 1))
         start(p2_copies(r, 1))
+        start(cc_copies(r, 1)[:1])
 
     def gather_end(r):
-        arrived(p2_copies(r, 0))
-        arrived(p2_copies(r, 1))
-        start([cc_copy(r)])
+        for flow in (0, 1):
+            lines = p2_copies(r, flow)
+            onward = cc_copies(r, flow)
+            for k in (0, 2, 1):
+                arrived([lines[k]])
+                start([onward[k + 1]])
 
     C2, C3A, C3B, D2, D3 = range(5)
 
@@ -282,61 +300,71 @@
     quarter = 0.25 / 16.0
 
     reduce_start(0)
+    relax_range(2, 0, 3)
+    x_sends[0][0].wait_send()
+    x_sends[0][1].wait_send()
+    x_sends[1][0].start()
+    arrived(x_sends[0])
+    correct(corr, (C2,), coef.at[0], [(quarter_x, halo, (0,))])
+    correct(corr, (C3B,), coef.at[1], [(quarter, corr, (C2,))])
+    correct(v, (3, 3), coef.at[2], [(quarter, corr, (C3B,))], add=True)
+    reduce_start(1)
     slow_send.wait_recv()
+    start(slow_shares)
+    gather_start(0)
+    x_sends[1][1].start()
+    gather_middle(0)
+    arrived(slow_shares)
     for g in range(2):
         cr, ci = coefs((0.12 * weights[g]) * slow_x[...])
         coef_x[g, 0] = cr
         coef_x[g, 1] = ci
     correct(corr, (D2,), coef_x, [(quarter, v, (0, 1))])
-    gather_start(0)
-
-    x_sends[0].wait_recv()
-    correct(corr, (C2,), coef.at[0], [(quarter_x, halo, (0,))])
-    correct(corr, (C3B,), coef.at[1], [(quarter, corr, (C2,))])
-    correct(v, (3, 3), coef.at[2], [(quarter, corr, (C3B,))], add=True)
-    reduce_start(1)
-    gather_middle(0)
     correct(corr, (D3,), coef_x, [(half, corr, (D2,)), (quarter, v, (1, 1)), (quarter, corr, (C2,))],
             minus=(corr, (D2,)))
-    gather_start(1)
-    gather_end(0)
-    gather_middle(1)
-
-    x_sends[1].wait_recv()
+    x_sends[1][0].wait_send()
+    x_sends[1][1].wait_send()
+    x_sends[2][0].start()
+    arrived(x_sends[1])
     correct(corr, (C3A,), coef.at[0],
             [(half, corr, (C2,)), (quarter_x, halo, (1,)), (quarter_x, corr, (D2,))],
             minus=(corr, (C2,)))
     correct(v, (3, 2), coef.at[1], [(half, corr, (C3B,)), (quarter, corr, (C3A,))],
             minus=(corr, (C3B,)), add=True)
     reduce_start(2)
+    x_sends[2][1].start()
     correct(v, (3, 1), coef.at[0],
             [(half, corr, (C3A,)), (quarter, corr, (C3B,)), (quarter_x, corr, (D3,))],
             minus=(corr, (C3A,)), add=True)
-    gather_end(1)
-    gather_start(2)
-    gather_middle(2)
-    gather_end(2)
-
-    x_sends[2].wait_recv()
+    gather_end(0)
+
+    arrived(x_sends[2])
     correct(v, (3, 1), coef.at[0], [(quarter_x, halo, (2,))], add=True)
     reduce_start(3)
-    gather_start(3)
-    gather_middle(3)
-    gather_end(3)
-    for r in range(4):
-        arrived([cc_copy(r)])
+    gather_start(1)
+    gather_start(2)
+    gather_middle(1)
+    gather_middle(2)
+    gather_end(1)
+    gather_end(2)
+    for r in range(len(GATHER)):
+        for flow in (0, 1):
+            arrived(cc_copies(r, flow))
 
     def pick(k, carry):
         tile = cover_ref[0, s, k]
-        o = tile // CX
-        j = lax.rem(tile, CX)
-        oc = lax.rem(o, 2)
+        o = lax.shift_right_logical(tile, 3)
+        j = tile & 7
+        oc = o & 1
         m = j + oc * (CX - 1 - 2 * j)
-        deliv_ref[0, 0, k] = ag[o // 16, lax.rem(o // 4, 4), lax.rem(o // 2, 2), oc, m]
+        deliv_ref[0, 0, k] = ag[
+            lax.shift_right_logical(o, 4), lax.shift_right_logical(o, 2) & 3,
+            lax.shift_right_logical(o, 1) & 1, oc, m,
+        ]
         return carry
-    lax.fori_loop(0, deliv_ref.shape[2], pick, 0)
-
-    for copy in x_sends + [slow_send] + c_sends + sent:
+    lax.fori_loop(0, deliv_ref.shape[2], pick, 0, unroll=8)
+
+    for copy in x_sends[2] + [slow_send] + c_sends + sent:
         copy.wait_send()
 
 
@@ -374,10 +402,10 @@
             vm((3, cx, 2, BAND, ny), f32),
             vm((4, 4, 2, 2, cx, BAND, ny), f32),
             dma((cx,)), dma((cx,)),
-            dma((3,)), dma((3,)), dma, dma, dma((3,)), dma((3,)),
+            dma((3, 2)), dma((3, 2)), dma((4,)), dma((4,)), dma((3,)), dma((3,)),
             dma((4, 3)), dma((4, 3)), dma((4,)), dma((4,)),
             dma((2, 4, 3)), dma((2, 4, 3)), dma((2, 4, 3)), dma((2, 4, 3)),
-            dma((4,)), dma((4,)),
+            dma((2, 4, 4)), dma((2, 4, 4)),
         ],
         compiler_params=pltpu.CompilerParams(
             collective_id=0, has_side_effects=True, vmem_limit_bytes=60 << 20

time: 185 us -> 140 us (0.76)
  Pallas kernels: 181 us -> 135 us
    pallas_call x1, Pallas kernels: 181 us -> 135 us  [body(): pl.pallas_call(kernel, name='inversion_step', out_shape=(jax.ShapeDtypeSt...]
where the time goes in v2:
time: 140 us; the launch traced here: 139 us
  Pallas kernels  135 us (96%)
  local copies, waits for them, and re-layouts  3.83 us (3%)
    pallas_call x1, Pallas kernels, body(): pl.pallas_call(kernel, name='inversion_step', out_shape=(jax.ShapeDtypeSt...  135 us
    unnamed x2, local copies, waits for them, and re-layouts  3.83 us

profile of v2, /device:TPU:1, one launch (start us, length us, event | category | flops | bytes accessed | tf_op | source)
XLA Modules:
  0.0 139.3 jit_solution(5924229973865636183)
XLA Ops:
  0.6 134.9 %inversion_step.1 = (f32[8,16,256]{2,1,0:T(8,128)}, f32[1,1,64,16,256]{4,3,2,1,0:T(8,128)}) custom-call(f32[2,4,8,64,256]{4,3,2,1,0:T(8,128)} %src_hbm.1, f32[8,64,256]{2,1,0:T(8,128)} %slow_hbm.1, s32[2]{0:T(128)} %freq_ref.1, s32[1,64,64]{2,1,0:T(8,128)} %cover_ref.1), custom_call_target="tpu_custom_call" | custom-call | tf_op jit(solution)/shard_map/inversion_step/pallas_call | solution.py:378
  135.5 1.6 %copy.8 = f32[8,16,256]{2,1,0:T(8,128)} copy(f32[8,16,256]{2,1,0:T(8,128)} %get-tuple-element.4) | data formatting | bytes 262144
  137.1 2.3 %copy.9 = f32[1,1,64,16,256]{4,3,2,1,0:T(8,128)} copy(f32[1,1,64,16,256]{4,3,2,1,0:T(8,128)} %get-tuple-element.5) | data formatting | bytes 2097152

commit v3 on v2

--- a/solution.py
+++ b/solution.py
@@ -26,7 +26,7 @@
 
 def kernel(
     src_hbm, slow_hbm, freq_ref, cover_ref, pre_ref, deliv_ref,
-    src, slow, coef, v, halo, slow_x, coef_x, corr, gi, rsr, ag,
+    src, slow, coef, v, halo, slow_x, coef_x, corr, gi, rsr, near, far, ag,
     load_sem, slow_sem, halo_ssem, halo_rsem, sx_ssem, sx_rsem, core_ssem, core_rsem,
     rs_ssem, rs_rsem, z_ssem, z_rsem, p1_ssem, p1_rsem, p2_ssem, p2_rsem, cc_ssem, cc_rsem,
 ):
@@ -49,6 +49,8 @@
     xs = [dev(lax.rem(x + k, 4), y, zh, c) for k in (1, 2, 3)]
     ys = [dev(x, lax.rem(y + k, 4), zh, c) for k in (1, 2, 3)]
     fs = [{"freq": lax.rem(f + k, 4), "sub": s} for k in (1, 2, 3)]
+    near_dev = {"freq": f + 1 - 2 * lax.rem(f, 2), "sub": s}
+    far_dev = fs[1]
     has_x = jnp.where((s == 0) | (s == 63), 0.0, 1.0).astype(jnp.float32)
     quarter_x = has_x * (0.25 / 16.0)
 
@@ -186,21 +188,45 @@
                     gg = weights[g] * (ur * ar - ui * ai)
                     ii = weights[g] * (ur * ur + ui * ui)
                     grad, illum = (gg, ii) if grad is None else (grad + gg, illum + ii)
-                gi[b, m, 0] = grad
-                gi[b, m, 1] = illum
+                gi[b // 2, b % 2, m, 0] = grad
+                gi[b // 2, b % 2, m, 1] = illum
             return carry
         lax.fori_loop(lo, hi, one, 0)
 
     sent = []
+
+    fj, fp = f // 2, lax.rem(f, 2)
 
     def rs_copies(r):
         lo, hi = REDUCE[r]
         n = pl.ds(lo, hi - lo)
-        return [
-            remote(gi.at[lax.rem(f + k + 1, 4), n], rsr.at[k, n],
-                   rs_ssem.at[r, k], rs_rsem.at[r, k], fs[k])
-            for k in range(3)
-        ]
+        out = []
+        for k in range(3):
+            to = lax.rem(f + k + 1, 4)
+            out.append(remote(gi.at[to // 2, lax.rem(to, 2), n], rsr.at[k, n],
+                              rs_ssem.at[r, k], rs_rsem.at[r, k], fs[k]))
+        return out
+
+    def near_copy(r):
+        lo, hi = REDUCE[r]
+        n = pl.ds(lo, hi - lo)
+        return remote(gi.at[:, 1 - fp, n], near.at[:, n], rs_ssem.at[r, 0], rs_rsem.at[r, 0], near_dev)
+
+    def far_copy(r):
+        lo, hi = REDUCE[r]
+        n = pl.ds(lo, hi - lo)
+        return remote(near.at[1 - fj, n], far.at[n], rs_ssem.at[r, 1], rs_rsem.at[r, 1], far_dev)
+
+    def reduce_far(r):
+        arrived([near_copy(r)])
+
+        def one(m, carry):
+            for part in range(2):
+                for j in range(2):
+                    near[j, m, part] = near[j, m, part] + gi[j, fp, m, part]
+            return carry
+        lax.fori_loop(*REDUCE[r], one, 0)
+        start([far_copy(r)])
 
     def block(r, *where):
         lo, hi = GATHER[r]
@@ -243,16 +269,24 @@
 
     def reduce_start(r):
         finish(*REDUCE[r])
-        start(rs_copies(r))
+        start([near_copy(r)] if r < 2 else rs_copies(r))
 
     def gather_start(r):
-        for i in (0, 1) if r == 0 else (r + 1,):
-            arrived(rs_copies(i))
         lo, hi = GATHER[r]
+        if r == 0:
+            arrived([far_copy(0)])
+            arrived([far_copy(1)])
+        else:
+            arrived(rs_copies(r + 1))
 
         def one(m, carry):
-            grad = gi[f, m, 0] + rsr[0, m, 0] + rsr[1, m, 0] + rsr[2, m, 0]
-            illum = gi[f, m, 1] + rsr[0, m, 1] + rsr[1, m, 1] + rsr[2, m, 1]
+            if r == 0:
+                grad, illum = [near[fj, m, part] + far[m, part] for part in range(2)]
+            else:
+                grad, illum = [
+                    gi[fj, fp, m, part] + rsr[0, m, part] + rsr[1, m, part] + rsr[2, m, part]
+                    for part in range(2)
+                ]
             pre = grad / jnp.sqrt(illum + 1.0)
             ag[x, y, zh, c, m] = pre
             pre_ref[layer(m)] = pre
@@ -303,7 +337,6 @@
     relax_range(2, 0, 3)
     x_sends[0][0].wait_send()
     x_sends[0][1].wait_send()
-    x_sends[1][0].start()
     arrived(x_sends[0])
     correct(corr, (C2,), coef.at[0], [(quarter_x, halo, (0,))])
     correct(corr, (C3B,), coef.at[1], [(quarter, corr, (C2,))])
@@ -311,7 +344,10 @@
     reduce_start(1)
     slow_send.wait_recv()
     start(slow_shares)
+    reduce_far(0)
+    reduce_far(1)
     gather_start(0)
+    x_sends[1][0].start()
     x_sends[1][1].start()
     gather_middle(0)
     arrived(slow_shares)
@@ -379,8 +415,8 @@
         kernel,
         name="inversion_step",
         out_shape=(
-            jax.ShapeDtypeStruct((cx, BAND, ny), f32),
-            jax.ShapeDtypeStruct((1, 1, tiles, BAND, ny), f32),
+            vm((cx, BAND, ny), f32),
+            vm((1, 1, tiles, BAND, ny), f32),
         ),
         in_specs=[
             pl.BlockSpec(memory_space=pl.ANY),
@@ -398,8 +434,10 @@
             vm((nz, ny), f32),
             vm((groups, 2, nz, ny), f32),
             vm((5,) + field, f32),
-            vm((4, cx, 2, BAND, ny), f32),
+            vm((2, 2, cx, 2, BAND, ny), f32),
             vm((3, cx, 2, BAND, ny), f32),
+            vm((2, cx, 2, BAND, ny), f32),
+            vm((cx, 2, BAND, ny), f32),
             vm((4, 4, 2, 2, cx, BAND, ny), f32),
             dma((cx,)), dma((cx,)),
             dma((3, 2)), dma((3, 2)), dma((4,)), dma((4,)), dma((3,)), dma((3,)),

time: 140 us -> 136 us (0.971)
  local copies, waits for them, and re-layouts: 3.83 us -> 1.63 us
    unnamed x2, local copies, waits for them, and re-layouts: 3.83 us -> 1.63 us
where the time goes in v3:
time: 136 us
  Pallas kernels  134 us (99%)
  local copies, waits for them, and re-layouts  1.63 us (1%)
    pallas_call x1, Pallas kernels, body(): pl.pallas_call(kernel, name='inversion_step', out_shape=(vm((cx, BAND, ny...  134 us

profile of v3, /device:TPU:1, one launch (start us, length us, event | category | flops | bytes accessed | tf_op | source)
XLA Modules:
  0.0 135.8 jit_solution(2843210978373444124)
XLA Ops:
  0.6 133.5 %inversion_step.1 = (f32[8,16,256]{2,1,0:T(8,128)S(1)}, f32[1,1,64,16,256]{4,3,2,1,0:T(8,128)S(1)}) custom-call(f32[2,4,8,64,256]{4,3,2,1,0:T(8,128)} %src_hbm.1, f32[8,64,256]{2,1,0:T(8,128)} %slow_hbm.1, s32[2]{0:T(128)} %freq_ref.1, s32[1,64,64]{2,1,0:T(8,128)} %cover_ref.1), custom_call_target="tpu_custom_call" | custom-call | tf_op jit(solution)/shard_map/inversion_step/pallas_call | solution.py:414
  134.2 0.7 copy.8
  134.8 1.0 copy.9

commit v4 on v3

--- a/solution.py
+++ b/solution.py
@@ -269,18 +269,18 @@
 
     def reduce_start(r):
         finish(*REDUCE[r])
-        start([near_copy(r)] if r < 2 else rs_copies(r))
+        start([near_copy(r)] if r < 1 else rs_copies(r))
 
     def gather_start(r):
         lo, hi = GATHER[r]
         if r == 0:
             arrived([far_copy(0)])
-            arrived([far_copy(1)])
+            arrived(rs_copies(1))
         else:
             arrived(rs_copies(r + 1))
 
-        def one(m, carry):
-            if r == 0:
+        def one(m, carry, summed=(r == 0)):
+            if summed:
                 grad, illum = [near[fj, m, part] + far[m, part] for part in range(2)]
             else:
                 grad, illum = [
@@ -291,6 +291,9 @@
             ag[x, y, zh, c, m] = pre
             pre_ref[layer(m)] = pre
             return carry
+        if r == 0:
+            one(2, 0, False)
+            lo = 3
         lax.fori_loop(lo, hi, one, 0)
         start([z_copy(r)])
         start(p1_copies(r, 0))
@@ -345,7 +348,6 @@
     slow_send.wait_recv()
     start(slow_shares)
     reduce_far(0)
-    reduce_far(1)
     gather_start(0)
     x_sends[1][0].start()
     x_sends[1][1].start()

time: 136 us -> 136 us (level)
  no operation moved by 1% of the time
where the time goes in v4:
time: 136 us
  Pallas kernels  133 us (98%)
  local copies, waits for them, and re-layouts  1.63 us (1%)
    pallas_call x1, Pallas kernels, body(): pl.pallas_call(kernel, name='inversion_step', out_shape=(vm((cx, BAND, ny...  133 us

profile of v4, /device:TPU:1, one launch (start us, length us, event | category | flops | bytes accessed | tf_op | source)
XLA Modules:
  0.0 135.6 jit_solution(2516397468602894635)
XLA Ops:
  0.6 133.3 %inversion_step.1 = (f32[8,16,256]{2,1,0:T(8,128)S(1)}, f32[1,1,64,16,256]{4,3,2,1,0:T(8,128)S(1)}) custom-call(f32[2,4,8,64,256]{4,3,2,1,0:T(8,128)} %src_hbm.1, f32[8,64,256]{2,1,0:T(8,128)} %slow_hbm.1, s32[2]{0:T(128)} %freq_ref.1, s32[1,64,64]{2,1,0:T(8,128)} %cover_ref.1), custom_call_target="tpu_custom_call" | custom-call | tf_op jit(solution)/shard_map/inversion_step/pallas_call | solution.py:416
  133.9 0.7 copy.8
  134.6 1.0 copy.9
